TPU v7x, 32 devices: a whole 2x2x4 slice. The times are simulated.
32 devices in a mesh: grp: 2 (over y), row: 4 (over z), head: 2 (over x), br: 2 (over core).
Axes of the slice: x: 2, y: 2, z: 4, core: 2. Of those that a mesh axis runs over, the one named last changes fastest.
Arguments:
- pair_acts: float32 [16, 8, 128], P(('grp', 'row', 'head')), parts along dimension 0, may hold values from -6 to 6
- alignment: float32 [64, 8, 256], P(('grp', 'br'), ('row', 'head')), parts along dimension 0, may hold values from -6 to 6
- align_mask: int32 [64, 8], P('grp', ('row', 'head')), parts along dimension 0, may hold values from 0 to 1
- residue_mask: int32 [16], P('grp'), parts along dimension 0, may hold values from 0 to 1, as said below
- align_gain: float32 [256], replicated, may hold values from 0.25 to 1.75
- outer_in: float32 [256, 64], replicated, may hold values from -0.375 to 0.375
- outer_out: float32 [1024, 128], replicated, may hold values from -1 to 1
- tri_gain: float32 [2, 128], replicated, may hold values from 0.25 to 1.75
- tri_in: float32 [2, 128, 4, 128], P(None, None, 'br'), may hold values from -5 to 5
- tri_bias: float32 [2, 128, 4], P(None, None, 'br'), may hold values from -0.5 to 0.5
- tri_out: float32 [2, 4, 32, 128], P(None, 'br'), may hold values from -0.5 to 0.5
- pair_cotangent: float32 [16, 8, 128], P(('grp', 'row', 'head')), parts along dimension 0, may hold values from -6 to 6
Outputs:
- pair_out: float32 [16, 8, 128], P(('grp', 'row', 'head')), parts along dimension 0
- pair_grad: float32 [16, 8, 128], P(('grp', 'row', 'head')), parts along dimension 0
There are 2 independent parts, one for each index of `grp`. A program takes and returns all parts, laid end to end along the dimension named above; an argument that names none is the same for every part. Nothing has to cross between parts.
Inputs may be any that keep to these rules, and one draw needn't show every extreme that they name: `residue_mask`: 1 at residue 0, and 0 at one or more residues; `align_mask`: 1 at every residue of sequence 0 of each part.
All inputs are finite; a program needn't handle non-finite values.
Results may differ from a plain program's by a relative error of at most 0.0003.
Values sent between devices are 32-bit elements; how exact they have to be, the bound alone decides.
A program may use at most 64 MiB of HBM per device.

v0:
```python
import jax
import jax.numpy as jnp
from jax import lax
from jax.sharding import PartitionSpec as P

OPC = 32


PRECISE = lax.Precision.HIGHEST
EPSILON = 1e-05
MASK_SHIFT = 1000000000.0


def normalize(values, scales):
    average = jnp.mean(values, axis=-1, keepdims=True)
    centred = values - average
    spread = jnp.mean(centred * centred, axis=-1, keepdims=True)
    return centred * lax.rsqrt(spread + EPSILON) * scales


def core_total(values):
    return lax.psum(values, "br")


def reorient(values):
    turned = jnp.swapaxes(values, 0, 1)
    return lax.all_to_all(turned, ("row", "head"), split_axis=0, concat_axis=1, tiled=True)


def prepare(values, scales, weight_in, weight_bias):
    normed = normalize(values, scales)
    projected = jnp.einsum("ijc,chd->ijhd", normed, weight_in, precision=PRECISE)
    bias_local = jnp.einsum("jkc,ch->hjk", normed, weight_bias, precision=PRECISE)
    return (projected, bias_local)


def attend(projected, bias_full, key_shift, weight_out):
    head_size = projected.shape[-1] // 4
    queries = projected[..., :head_size]
    key_proj = projected[..., head_size : 2 * head_size]
    value_proj = projected[..., 2 * head_size : 3 * head_size]
    gating = projected[..., 3 * head_size :]
    logits = jnp.einsum("ijhd,ikhd->ihjk", queries, key_proj, precision=PRECISE) * head_size ** (
        -0.5
    )
    logits = logits + bias_full[None] + key_shift
    attention = jax.nn.softmax(logits, axis=-1)
    attended = jnp.einsum("ihjk,ikhd->ijhd", attention, value_proj, precision=PRECISE)
    gated_out = jax.nn.sigmoid(gating) * attended
    return jnp.einsum("ijhd,hdc->ijc", gated_out, weight_out, precision=PRECISE)


def tri_forward(rows_in, scales, weight_in, weight_bias, weight_out, key_shift, pair_mask):

    def local_prep(values):
        return prepare(values, scales, weight_in, weight_bias)

    (projected, bias_local), pull_prep = jax.vjp(local_prep, rows_in)
    bias_full = lax.all_gather(bias_local, ("row", "head"), axis=1, tiled=True)

    def local_attend(proj_in, bias_in):
        return attend(proj_in, bias_in, key_shift, weight_out)

    partial_out, pull_attend = jax.vjp(local_attend, projected, bias_full)
    total_out = core_total(partial_out)
    return (rows_in + total_out * pair_mask, (pull_prep, pull_attend))


def tri_backward(grad_out, saved, pair_mask):
    pull_prep, pull_attend = saved
    grad_proj, grad_bias = pull_attend(grad_out * pair_mask)
    grad_local = lax.psum_scatter(grad_bias, ("row", "head"), scatter_dimension=1, tiled=True)
    (grad_rows,) = pull_prep((grad_proj, grad_local))
    return grad_out + core_total(grad_rows)


def body(
    pair_acts,
    alignment,
    align_mask,
    residue_mask,
    align_gain,
    outer_in,
    outer_out,
    tri_gain,
    tri_in,
    tri_bias,
    tri_out,
    pair_cotangent,
):
    row_count = pair_acts.shape[0]
    live = residue_mask.astype(jnp.float32)
    key_shift = (live - 1.0) * MASK_SHIFT
    row_live = lax.dynamic_slice_in_dim(
        live, lax.axis_index(("row", "head")) * row_count, row_count, 0
    )
    pair_mask = row_live[:, None, None] * live[None, :, None]
    seq_count = alignment.shape[0]
    mask_all = align_mask.astype(jnp.float32)
    mask_own = lax.dynamic_slice_in_dim(mask_all, lax.axis_index("br") * seq_count, seq_count, 0)
    normed = normalize(alignment, align_gain)
    projected = jnp.einsum("snc,ck->snk", normed, outer_in, precision=PRECISE)
    left_part = projected[..., :OPC] * mask_own[..., None]
    right_part = jnp.swapaxes(projected[..., OPC:] * mask_own[..., None], 1, 2)
    right_all, mask_cols = (
        lax.all_gather(right_part, ("row", "head"), axis=2, tiled=True),
        lax.all_gather(mask_all, ("row", "head"), axis=1, tiled=True),
    )
    counts = jnp.einsum("si,sj->ij", mask_all, mask_cols, precision=PRECISE)
    table = outer_out.reshape(OPC, OPC, outer_out.shape[-1])
    mixed_left = jnp.einsum("sip,pqc->siqc", left_part, table, precision=PRECISE)
    partial_outer = jnp.einsum("siqc,sqj->ijc", mixed_left, right_all, precision=PRECISE)
    outer_sum = core_total(partial_outer)
    pair_one = pair_acts + outer_sum / counts[..., None]
    pair_two, saved_start = tri_forward(
        pair_one, tri_gain[0], tri_in[0], tri_bias[0], tri_out[0], key_shift, pair_mask
    )
    turned_two = reorient(pair_two)
    turned_three, saved_end = tri_forward(
        turned_two, tri_gain[1], tri_in[1], tri_bias[1], tri_out[1], key_shift, pair_mask
    )
    pair_out = reorient(turned_three)
    grad_turned = reorient(pair_cotangent)
    grad_turned = tri_backward(grad_turned, saved_end, pair_mask)
    grad_two = reorient(grad_turned)
    pair_grad = tri_backward(grad_two, saved_start, pair_mask)
    return (pair_out, pair_grad)


def solution(mesh):
    in_specs = (
        P(("grp", "row", "head"), None, None),
        P(("grp", "br"), ("row", "head"), None),
        P("grp", ("row", "head")),
        P("grp"),
        P(),
        P(),
        P(),
        P(),
        P(None, None, "br", None),
        P(None, None, "br"),
        P(None, "br", None, None),
        P(("grp", "row", "head"), None, None),
    )
    out_specs = (P(("grp", "row", "head"), None, None), P(("grp", "row", "head"), None, None))
    return jax.shard_map(body, mesh=mesh, in_specs=in_specs, out_specs=out_specs, check_vma=False)
```

profile of v0, /device:TPU:0, one launch (start us, length us, event | category | flops | bytes accessed | tf_op | source)
XLA Modules:
  0.0 188.4 jit_solution(10134027815885279675)
XLA Ops:
  0.7 1.0 reduce_sum.121
  2.0 0.7 convert_bitcast_fusion
  2.6 0.8 multiply_multiply_fusion
  3.7 32.3 %all_gather.12 = f32[16,32,8]{1,0,2:T(8,128)S(1)} all-gather(f32[16,32,1]{1,0,2:T(8,128)S(1)} %fusion.30), channel_id=1, replica_groups=mesh['grp'=2,'row'=4,'head'=2,'br'=2] {'row','head'}, dimensions={2}, use_global_device_ids=true | all-gather | bytes 18432 | tf_op jit(solution)/shard_map/all_gather | solution.py:106
  36.2 0.7 fusion.8
  36.9 0.7 convolution_bitcast_fusion.17
  37.6 2.5 %psum.35 = f32[1,8,128]{2,1,0:T(8,128)S(1)} all-reduce(f32[1,8,128]{2,1,0:T(8,128)S(1)} %convolution_bitcast_fusion.17), channel_id=1, replica_groups=mesh['grp'=2,'row'=4,'head'=2,'br'=2] {'br'}, use_global_device_ids=true, to_apply=%region_2.0 | all-reduce | flops 1024 | bytes 8192 | tf_op jit(solution)/shard_map/psum | solution.py:22
  40.0 20.4 %all-gather.2 = f32[8,1,32]{2,1,0:T(1,128)S(1)} all-gather(f32[1,1,32]{2,1,0:T(1,128)S(1)} %get-tuple-element.16), channel_id=1, replica_groups=mesh['grp'=2,'row'=4,'head'=2,'br'=2] {'row','head'}, dimensions={0}, use_global_device_ids=true | all-gather | bytes 1152 | tf_op jit(solution)/shard_map/all_gather | solution.py:107
  60.5 0.7 copy-done.8
  61.3 0.6 copy-done.7
  62.4 0.6 copy-done.9
  63.6 0.6 broadcast_multiply_fusion.2
  65.1 16.3 %all-gather.3 = f32[8,8,2]{1,2,0:T(2,128)S(1)} all-gather(f32[1,8,2]{1,2,0:T(2,128)S(1)} %convolution_bitcast_fusion.19), channel_id=2, replica_groups=mesh['grp'=2,'row'=4,'head'=2,'br'=2] {'row','head'}, dimensions={0}, use_global_device_ids=true | all-gather | bytes 576 | tf_op jit(solution)/shard_map/all_gather | solution.py:59
  82.8 2.5 %psum.36 = f32[1,8,128]{2,1,0:T(8,128)S(1)} all-reduce(f32[1,8,128]{2,1,0:T(8,128)S(1)} %convolution_bitcast_fusion.16), channel_id=1, replica_groups=mesh['grp'=2,'row'=4,'head'=2,'br'=2] {'br'}, use_global_device_ids=true, to_apply=%region_7.0 | all-reduce | flops 1024 | bytes 8192 | tf_op jit(solution)/shard_map/psum | solution.py:22
  85.2 0.7 multiply_add_fusion
  85.9 3.3 %all-to-all-start = ((f32[8,1,128]{2,1,0:T(1,128)}), f32[8,1,128]{2,1,0:T(1,128)S(1)}, u32[]{:S(2)}, u32[]{:S(2)}) async-start(f32[8,1,128]{2,1,0:T(1,128)} %bitcast.32), calls=%async_computation | async-start | bytes 8192 | tf_op jit(solution)/shard_map/all_to_all | solution.py:27
  89.3 0.6 copy-done.10
  90.5 5.1 %all-to-all-done = f32[8,1,128]{2,1,0:T(1,128)S(1)} async-done(((f32[8,1,128]{2,1,0:T(1,128)}), f32[8,1,128]{2,1,0:T(1,128)S(1)}, u32[]{:S(2)}, u32[]{:S(2)}) %all-to-all-start) | async-done | bytes 4128 | tf_op jit(solution)/shard_map/all_to_all | solution.py:27
  95.6 3.3 %all-to-all-start.2 = ((f32[8,1,128]{2,1,0:T(1,128)}), f32[8,1,128]{2,1,0:T(1,128)S(1)}, u32[]{:S(2)}, u32[]{:S(2)}) async-start(f32[8,1,128]{2,1,0:T(1,128)} %bitcast.54), calls=%async_computation.2 | async-start | bytes 8192 | tf_op jit(solution)/shard_map/all_to_all | solution.py:27
  99.5 20.9 %all-gather.4 = f32[8,8,2]{1,2,0:T(2,128)S(1)} all-gather(f32[1,8,2]{1,2,0:T(2,128)S(1)} %convolution_bitcast_fusion.18), channel_id=3, replica_groups=mesh['grp'=2,'row'=4,'head'=2,'br'=2] {'row','head'}, dimensions={0}, use_global_device_ids=true | all-gather | bytes 576 | tf_op jit(solution)/shard_map/all_gather | solution.py:59
  122.7 17.4 %all-reduce.8 = f32[2,8,8]{2,0,1:T(2,128)S(1)} all-reduce(f32[2,8,8]{2,0,1:T(2,128)S(1)} %copy.49), channel_id=4, replica_groups=mesh['grp'=2,'row'=4,'head'=2,'br'=2] {'row','head'}, use_global_device_ids=true, to_apply=%region_14.0.clone | all-reduce | flops 128 | bytes 1024
  140.0 0.8 fusion.92
  141.6 2.5 %psum.38 = f32[1,8,128]{2,1,0:T(8,128)S(1)} all-reduce(f32[1,8,128]{2,1,0:T(8,128)S(1)} %add_bitcast_fusion), channel_id=1, replica_groups=mesh['grp'=2,'row'=4,'head'=2,'br'=2] {'br'}, use_global_device_ids=true, to_apply=%region_17.0 | all-reduce | flops 1024 | bytes 8192 | tf_op jit(solution)/shard_map/psum | solution.py:22
  144.0 0.6 bitcast_add_fusion.1
  144.6 3.3 %all-to-all-start.3 = ((f32[8,1,128]{2,1,0:T(1,128)}), f32[8,1,128]{2,1,0:T(1,128)S(1)}, u32[]{:S(2)}, u32[]{:S(2)}) async-start(f32[8,1,128]{2,1,0:T(1,128)} %bitcast.75), calls=%async_computation.3 | async-start | bytes 8192 | tf_op jit(solution)/shard_map/all_to_all | solution.py:27
  148.2 6.1 %all-to-all-done.3 = f32[8,1,128]{2,1,0:T(1,128)S(1)} async-done(((f32[8,1,128]{2,1,0:T(1,128)}), f32[8,1,128]{2,1,0:T(1,128)S(1)}, u32[]{:S(2)}, u32[]{:S(2)}) %all-to-all-start.3) | async-done | bytes 4128 | tf_op jit(solution)/shard_map/all_to_all | solution.py:27
  155.6 17.9 %all-reduce.9 = f32[2,8,8]{2,0,1:T(2,128)S(1)} all-reduce(f32[2,8,8]{2,0,1:T(2,128)S(1)} %copy.52), channel_id=5, replica_groups=mesh['grp'=2,'row'=4,'head'=2,'br'=2] {'row','head'}, use_global_device_ids=true, to_apply=%region_19.0.clone | all-reduce | flops 128 | bytes 1024
  173.5 0.8 fusion.91
  175.1 2.5 %all-reduce.10 = (f32[1,8,128]{2,1,0:T(8,128)S(1)}, f32[1,8,128]{2,1,0:T(8,128)S(1)}) all-reduce(f32[1,8,128]{2,1,0:T(8,128)S(1)} %convolution_bitcast_fusion.15, f32[1,8,128]{2,1,0:T(8,128)S(1)} %broadcast_add_fusion), channel_id=1, replica_groups=mesh['grp'=2,'row'=4,'head'=2,'br'=2] {'br'}, use_global_device_ids=true, to_apply=%region_12.0 | all-reduce | flops 2048 | bytes 16384 | tf_op jit(solution)/shard_map/psum | solution.py:22
  177.5 0.7 bitcast_add_fusion.2
  178.2 3.3 %all-to-all-start.1 = ((f32[8,1,128]{2,1,0:T(1,128)}), f32[8,1,128]{2,1,0:T(1,128)S(1)}, u32[]{:S(2)}, u32[]{:S(2)}) async-start(f32[8,1,128]{2,1,0:T(1,128)} %bitcast.52), calls=%async_computation.1 | async-start | bytes 8192 | tf_op jit(solution)/shard_map/all_to_all | solution.py:27
  182.1 5.8 %all-to-all-done.1 = f32[8,1,128]{2,1,0:T(1,128)S(1)} async-done(((f32[8,1,128]{2,1,0:T(1,128)}), f32[8,1,128]{2,1,0:T(1,128)S(1)}, u32[]{:S(2)}, u32[]{:S(2)}) %all-to-all-start.1) | async-done | bytes 4128 | tf_op jit(solution)/shard_map/all_to_all | solution.py:27
  (93 shorter events, 11.5 us)
Async XLA Ops:
  0.6 35.6 %copy-start = (f32[1024,128]{1,0:T(8,128)S(1)}, f32[1024,128]{1,0:T(8,128)}, u32[]{:S(2)}) copy-start(f32[1024,128]{1,0:T(8,128)} %param.18) | copy-start | bytes 1572868
  0.6 1.0 copy-start.3
  0.7 2.8 %copy-start.4 = (f32[256,64]{0,1:T(8,128)S(1)}, f32[256,64]{0,1:T(8,128)}, u32[]{:S(2)}) copy-start(f32[256,64]{0,1:T(8,128)} %param.17) | copy-start | bytes 196612
  36.9 24.4 %copy-start.1 = (f32[2,128,2,128]{3,2,1,0:T(2,128)S(1)}, f32[2,128,2,128]{3,2,1,0:T(2,128)}, u32[]{:S(2)}) copy-start(f32[2,128,2,128]{3,2,1,0:T(2,128)} %param.20) | copy-start | bytes 786436
  60.5 0.7 copy-start.8
  61.2 0.7 copy-start.7
  61.2 0.7 copy-start.6
  62.3 0.7 copy-start.9
  64.2 0.7 copy-start.5
  81.7 0.8 copy-start.2
  85.9 9.7 %all-to-all-start = ((f32[8,1,128]{2,1,0:T(1,128)}), f32[8,1,128]{2,1,0:T(1,128)S(1)}, u32[]{:S(2)}, u32[]{:S(2)}) async-start(f32[8,1,128]{2,1,0:T(1,128)} %bitcast.32), calls=%async_computation | async-start | bytes 8192 | tf_op jit(solution)/shard_map/all_to_all | solution.py:27
  89.2 0.7 copy-start.10
  95.6 25.7 %all-to-all-start.2 = ((f32[8,1,128]{2,1,0:T(1,128)}), f32[8,1,128]{2,1,0:T(1,128)S(1)}, u32[]{:S(2)}, u32[]{:S(2)}) async-start(f32[8,1,128]{2,1,0:T(1,128)} %bitcast.54), calls=%async_computation.2 | async-start | bytes 8192 | tf_op jit(solution)/shard_map/all_to_all | solution.py:27
  144.6 9.7 %all-to-all-start.3 = ((f32[8,1,128]{2,1,0:T(1,128)}), f32[8,1,128]{2,1,0:T(1,128)S(1)}, u32[]{:S(2)}, u32[]{:S(2)}) async-start(f32[8,1,128]{2,1,0:T(1,128)} %bitcast.75), calls=%async_computation.3 | async-start | bytes 8192 | tf_op jit(solution)/shard_map/all_to_all | solution.py:27
  178.2 9.7 %all-to-all-start.1 = ((f32[8,1,128]{2,1,0:T(1,128)}), f32[8,1,128]{2,1,0:T(1,128)S(1)}, u32[]{:S(2)}, u32[]{:S(2)}) async-start(f32[8,1,128]{2,1,0:T(1,128)} %bitcast.52), calls=%async_computation.1 | async-start | bytes 8192 | tf_op jit(solution)/shard_map/all_to_all | solution.py:27
where the time goes:
time: 189 us; the launch traced here: 188 us
  blocking collectives  135 us (71%)
  waiting for transfers between devices  17 us (9%)
  starting transfers between devices  13.2 us (7%)
  matrix products  8.39 us (4%)
  other arithmetic  7.59 us (4%)
  local copies, waits for them, and re-layouts  6.07 us (3%)
    all_gather x2, blocking collectives, tri_forward(): bias_full = lax.all_gather(bias_local, ('row', 'head'), axis=1, tiled=True)  37.2 us
    unnamed x2, blocking collectives  35.3 us
    all_gather x1, blocking collectives, body(): lax.all_gather(right_part, ('row', 'head'), axis=2, tiled=True)  32.3 us
    all_gather x1, blocking collectives, body(): lax.all_gather(mask_all, ('row', 'head'), axis=1, tiled=True)  20.4 us
    all_to_all x4, waiting for transfers between devices, reorient(): lax.all_to_all(turned, ('row', 'head'), split_axis=0, concat_axis=1, tile...  17 us
    all_to_all x4, starting transfers between devices, reorient(): lax.all_to_all(turned, ('row', 'head'), split_axis=0, concat_axis=1, tile...  13.2 us
    psum x4, blocking collectives, core_total(): return lax.psum(values, 'br')  9.82 us
    unnamed x26, local copies, waits for them, and re-layouts  4.8 us
  transfers between devices with their start and end apart: 4, of which 3 were waited for; matrix products, arithmetic and copies ran while one was open for 2% of the time, Pallas kernels for 0%

commit v1 on v0

--- a/solution.py
+++ b/solution.py
@@ -1,6 +1,10 @@
+import functools
+
 import jax
 import jax.numpy as jnp
 from jax import lax
+from jax.experimental import pallas as pl
+from jax.experimental.pallas import tpu as pltpu
 from jax.sharding import PartitionSpec as P
 
 OPC = 32
@@ -74,7 +78,7 @@
     return grad_out + core_total(grad_rows)
 
 
-def body(
+def spread_body(
     pair_acts,
     alignment,
     align_mask,
@@ -127,6 +131,533 @@
     return (pair_out, pair_grad)
 
 
+MESH_ID = pl.DeviceIdType.MESH
+FUSED_BYTES = 1 << 20
+NN = ((1,), (0,))
+NT = ((1,), (1,))
+TN = ((0,), (0,))
+
+
+def split(values):
+    high = values.astype(jnp.bfloat16)
+    low = (values - high.astype(jnp.float32)).astype(jnp.bfloat16)
+    return (high, low)
+
+
+def pair_dot(first, second, dims):
+    def one(a, b):
+        return lax.dot_general(a, b, (dims, ((), ())), preferred_element_type=jnp.float32)
+
+    return one(first[0], second[0]) + (one(first[0], second[1]) + one(first[1], second[0]))
+
+
+def standardize(values):
+    average = jnp.mean(values, axis=-1, keepdims=True)
+    centred = values - average
+    spread = jnp.mean(centred * centred, axis=-1, keepdims=True)
+    inverse = lax.rsqrt(spread + EPSILON)
+    return (centred * inverse, inverse)
+
+
+def fused_kernel(
+    sizes,
+    live_ref,
+    acts_hbm,
+    align_hbm,
+    mask_hbm,
+    gain_hbm,
+    outer_in_hbm,
+    outer_out_hbm,
+    tri_gain_hbm,
+    tri_in_hbm,
+    tri_bias_hbm,
+    tri_out_hbm,
+    cot_hbm,
+    out_ref,
+    grad_ref,
+    acts_all,
+    cot_all,
+    proj_all,
+    align_v,
+    mask_v,
+    gain_v,
+    outer_in_v,
+    outer_out_v,
+    tri_gain_v,
+    tri_in_all,
+    tri_bias_all,
+    tri_out_all,
+    table_hi,
+    table_lo,
+    wide_hi,
+    wide_lo,
+    turn_v,
+    mixed_v,
+    load_sems,
+    send_acts,
+    recv_acts,
+    send_proj,
+    recv_proj,
+    send_cot,
+    recv_cot,
+    send_w,
+    recv_w,
+):
+    rows_n, heads_n, cores_n = sizes
+    count = rows_n * heads_n
+    chan = acts_all.shape[-1]
+    my_row = lax.axis_index("row")
+    my_head = lax.axis_index("head")
+    my_core = lax.axis_index("br")
+    me = my_row * heads_n + my_head
+    seqs = align_v.shape[0]
+    half = tri_in_all.shape[3]
+    head_count = half * cores_n
+    size = tri_in_all.shape[4] // 4
+    width = head_count * size
+
+    peers = [
+        (dr, dh, db)
+        for dr in range(rows_n)
+        for dh in range(heads_n)
+        for db in range(cores_n)
+        if (dr, dh, db) != (0, 0, 0)
+    ]
+
+    def place(offset):
+        dr, dh, db = offset
+        return (
+            lax.rem(my_row + dr, rows_n),
+            lax.rem(my_head + dh, heads_n),
+            lax.rem(my_core + db, cores_n),
+        )
+
+    def target(offset):
+        row, head, core = place(offset)
+        return {"row": row, "head": head, "br": core}
+
+    barrier = pltpu.get_barrier_semaphore()
+    for offset in peers:
+        pl.semaphore_signal(barrier, inc=1, device_id=target(offset), device_id_type=MESH_ID)
+
+    loads = [
+        pltpu.make_async_copy(align_hbm, align_v, load_sems.at[0]),
+        pltpu.make_async_copy(gain_hbm, gain_v, load_sems.at[1]),
+        pltpu.make_async_copy(outer_in_hbm, outer_in_v, load_sems.at[2]),
+        pltpu.make_async_copy(mask_hbm, mask_v, load_sems.at[3]),
+        pltpu.make_async_copy(acts_hbm.at[0], acts_all.at[me, 0:count], load_sems.at[4]),
+        pltpu.make_async_copy(tri_in_hbm, tri_in_all.at[my_core], load_sems.at[5]),
+        pltpu.make_async_copy(tri_bias_hbm, tri_bias_all.at[my_core], load_sems.at[6]),
+        pltpu.make_async_copy(tri_out_hbm, tri_out_all.at[my_core], load_sems.at[7]),
+        pltpu.make_async_copy(cot_hbm.at[0], cot_all.at[me], load_sems.at[8]),
+        pltpu.make_async_copy(outer_out_hbm, outer_out_v, load_sems.at[9]),
+        pltpu.make_async_copy(tri_gain_hbm, tri_gain_v, load_sems.at[10]),
+    ]
+    for load in loads:
+        load.start()
+    for load in loads[:4]:
+        load.wait()
+
+    aligned = align_v[:, 0, :]
+    normed = standardize(aligned)[0] * gain_v[...]
+    projected = pair_dot(split(normed), split(outer_in_v[...]), NN)
+    mask_f = mask_v[...].astype(jnp.float32)
+    lo_seq = mask_f[0:seqs]
+    mask_own = lo_seq
+    for core in range(1, cores_n):
+        mask_own = jnp.where(my_core == core, mask_f[core * seqs : (core + 1) * seqs], mask_own)
+    projected = projected * mask_own
+    pieces = seqs // 8
+    proj_all[my_core, me] = jnp.concatenate(
+        [projected[8 * piece : 8 * piece + 8] for piece in range(pieces)], axis=1
+    )
+    depth = mask_f.shape[0]
+    lane = lax.broadcasted_iota(jnp.int32, (depth, chan), 1)
+    place_s = lax.broadcasted_iota(jnp.int32, (depth, chan), 0)
+    mask_row = jnp.sum(jnp.where(lane == place_s, mask_f, 0.0), axis=0, keepdims=True)
+    acts_all[me, count : count + 1] = mask_row
+    for load in loads[4:]:
+        load.wait()
+
+    pl.semaphore_wait(barrier, len(peers))
+
+    sends = []
+    receives = []
+    weight_receives = []
+    cot_receives = []
+
+    def remote(src, dst, send_sem, recv_sem, offset):
+        return pltpu.make_async_remote_copy(
+            src_ref=src,
+            dst_ref=dst,
+            send_sem=send_sem,
+            recv_sem=recv_sem,
+            device_id=target(offset),
+            device_id_type=MESH_ID,
+        )
+
+    ordered = sorted(peers, key=lambda o: -(min(o[0], rows_n - o[0]) + o[1]))
+    for number, offset in enumerate(ordered):
+        row, head, core = place(offset)
+        other = row * heads_n + head
+        copy = remote(
+            proj_all.at[my_core, me],
+            proj_all.at[my_core, me],
+            send_proj.at[number],
+            recv_proj.at[my_core, me],
+            offset,
+        )
+        copy.start()
+        sends.append(copy)
+        receives.append(
+            remote(
+                proj_all.at[core, other],
+                proj_all.at[core, other],
+                send_proj.at[number],
+                recv_proj.at[core, other],
+                offset,
+            )
+        )
+        if offset[2] == 0:
+            copy = remote(
+                acts_all.at[me, 0 : count + 1],
+                acts_all.at[me, 0 : count + 1],
+                send_acts.at[number],
+                recv_acts.at[me],
+                offset,
+            )
+            copy.start()
+            sends.append(copy)
+            receives.append(
+                remote(
+                    acts_all.at[other, 0 : count + 1],
+                    acts_all.at[other, 0 : count + 1],
+                    send_acts.at[number],
+                    recv_acts.at[other],
+                    offset,
+                )
+            )
+    for db in range(1, cores_n):
+        offset = (0, 0, db)
+        core = lax.rem(my_core + db, cores_n)
+        for which, ref in enumerate((tri_in_all, tri_bias_all, tri_out_all)):
+            copy = remote(
+                ref.at[my_core],
+                ref.at[my_core],
+                send_w.at[which, db],
+                recv_w.at[which, my_core],
+                offset,
+            )
+            copy.start()
+            sends.append(copy)
+            weight_receives.append(
+                remote(
+                    ref.at[core],
+                    ref.at[core],
+                    send_w.at[which, db],
+                    recv_w.at[which, core],
+                    offset,
+                )
+            )
+    for number, offset in enumerate(ordered):
+        if offset[2] == 0:
+            row, head, core = place(offset)
+            other = row * heads_n + head
+            copy = remote(
+                cot_all.at[me], cot_all.at[me], send_cot.at[number], recv_cot.at[me], offset
+            )
+            copy.start()
+            sends.append(copy)
+            cot_receives.append(
+                remote(
+                    cot_all.at[other],
+                    cot_all.at[other],
+                    send_cot.at[number],
+                    recv_cot.at[other],
+                    offset,
+                )
+            )
+
+    for q in range(OPC):
+        high, low = split(outer_out_v[pl.ds(q, OPC, stride=OPC), :])
+        table_hi[q * OPC : (q + 1) * OPC] = high
+        table_lo[q * OPC : (q + 1) * OPC] = low
+
+    pairs = count * count
+    lanes = head_count * pairs
+    tile_row = lax.broadcasted_iota(jnp.int32, (count, count, lanes), 0)
+    lane_at = lax.rem(lax.broadcasted_iota(jnp.int32, (count, count, lanes), 2), pairs)
+    at_first = tile_row == lane_at // count
+    at_second = tile_row == lax.rem(lane_at, count)
+    live = [live_ref[n].astype(jnp.float32) for n in range(count)]
+    key_at = lax.broadcasted_iota(jnp.int32, (count, lanes), 0)
+    first_at = lax.broadcasted_iota(jnp.int32, (count, count, chan), 0)
+    second_at = lax.broadcasted_iota(jnp.int32, (count, count, chan), 1)
+    key_live = jnp.zeros((count, lanes), jnp.float32)
+    live_first = jnp.zeros((count, count, chan), jnp.float32)
+    live_second = jnp.zeros((count, count, chan), jnp.float32)
+    for n in range(count):
+        key_live = jnp.where(key_at == n, live[n], key_live)
+        live_first = jnp.where(first_at == n, live[n], live_first)
+        live_second = jnp.where(second_at == n, live[n], live_second)
+    key_shift = (key_live - 1.0) * MASK_SHIFT
+    pair_mask = (live_first * live_second).reshape(pairs, chan)
+    lane_head = lax.broadcasted_iota(jnp.int32, (pairs, width), 1) // size
+
+    def heads_apart(values):
+        return jnp.concatenate(
+            [jnp.where(lane_head == h, values, 0.0) for h in range(head_count)], axis=0
+        )
+
+    def heads_together(values):
+        total = jnp.where(lane_head == 0, values[0:pairs], 0.0)
+        for h in range(1, head_count):
+            total = jnp.where(lane_head == h, values[h * pairs : (h + 1) * pairs], total)
+        return total
+
+    def spread_over(values, where):
+        return jnp.where(where, values[None], 0.0).reshape(pairs, lanes)
+
+    def fold(values, where):
+        return jnp.sum(jnp.where(where, values.reshape(count, count, lanes), 0.0), axis=0)
+
+    for receive in weight_receives:
+        receive.wait_recv()
+
+    outs = []
+    for t in range(2):
+        blocks = []
+        for h in range(head_count):
+            blocks.append(tri_in_all[h // half, t, :, h % half, :])
+        for block in range(4):
+            columns = jnp.concatenate(
+                [b[:, block * size : (block + 1) * size] for b in blocks], axis=1
+            )
+            high, low = split(columns)
+            wide_hi[t, :, block * width : (block + 1) * width] = high
+            wide_lo[t, :, block * width : (block + 1) * width] = low
+        bias_columns = jnp.concatenate(
+            [
+                jnp.broadcast_to(
+                    tri_bias_all[h // half, t, :, h % half : h % half + 1], (chan, pairs)
+                )
+                for h in range(head_count)
+            ],
+            axis=1,
+        )
+        high, low = split(bias_columns)
+        wide_hi[t, :, 4 * width :] = high
+        wide_lo[t, :, 4 * width :] = low
+        outs.append(
+            split(
+                jnp.concatenate(
+                    [tri_out_all[h // half, t, h % half] for h in range(head_count)], axis=0
+                )
+            )
+        )
+
+    for receive in receives:
+        receive.wait_recv()
+
+    left_tiles = []
+    right_tiles = []
+    for core in range(cores_n):
+        for piece in range(pieces):
+            base = piece * 2 * OPC
+            left_tiles.append(
+                jnp.concatenate(
+                    [proj_all[core, n, :, base : base + OPC] for n in range(count)], axis=1
+                )
+            )
+            right_tiles.append(
+                jnp.concatenate(
+                    [proj_all[core, n, :, base + OPC : base + 2 * OPC] for n in range(count)],
+                    axis=1,
+                )
+            )
+    left = jnp.concatenate(left_tiles, axis=0)
+    right = jnp.concatenate(right_tiles, axis=0)
+    mixed = pair_dot(split(right), split(left), TN)
+    for block in range(mixed_v.shape[0]):
+        mixed_v[block] = mixed[:, block * chan : (block + 1) * chan]
+    strips = [[] for _ in range(count)]
+    for q in range(OPC):
+        for block in range(mixed_v.shape[0]):
+            tile = mixed_v[block, pl.ds(q, count, stride=OPC), :]
+            for n in range(chan // OPC):
+                strips[block * (chan // OPC) + n].append(tile[:, n * OPC : (n + 1) * OPC])
+    crossed = jnp.concatenate([jnp.concatenate(s, axis=1) for s in strips], axis=0)
+    summed = pair_dot(split(crossed), (table_hi[...], table_lo[...]), NN)
+    mask_rows = jnp.concatenate([acts_all[n, count : count + 1] for n in range(count)], axis=0)
+    counts = jnp.sum(mask_rows[:, None, :] * mask_rows[None, :, :], axis=-1, keepdims=True)
+    acts = jnp.concatenate([acts_all[n, 0:count] for n in range(count)], axis=0)
+    pair_one = acts + summed / counts.reshape(pairs, 1)
+
+    def turn(values):
+        turn_v[...] = values
+        return jnp.concatenate(
+            [turn_v[pl.ds(n, count, stride=count), :] for n in range(count)], axis=0
+        )
+
+    scale = size ** (-0.5)
+
+    def forward(x, t):
+        gain = tri_gain_v[t : t + 1]
+        hat, inverse = standardize(x)
+        weights = (wide_hi[t], wide_lo[t])
+        projected = pair_dot(split(hat * gain), weights, NN)
+        query = projected[:, 0:width] * scale
+        key = split(projected[:, width : 2 * width])
+        value = split(projected[:, 2 * width : 3 * width])
+        gate = jax.nn.sigmoid(projected[:, 3 * width : 4 * width])
+        bias = fold(projected[:, 4 * width :], at_second)
+        query_apart = split(heads_apart(query))
+        logits = fold(pair_dot(key, query_apart, NT), at_first) + bias + key_shift
+        top = jnp.max(logits, axis=0, keepdims=True)
+        exps = jnp.exp(logits - top)
+        probs = exps / jnp.sum(exps, axis=0, keepdims=True)
+        probs_wide = split(spread_over(probs, at_first))
+        attended = heads_together(pair_dot(probs_wide, value, TN))
+        update = pair_dot(split(gate * attended), outs[t], NN)
+        saved = (hat, inverse, gain, weights, key, value, gate, query_apart, probs, probs_wide, attended)
+        return (x + update * pair_mask, saved)
+
+    def backward(grad, t, saved):
+        hat, inverse, gain, weights, key, value, gate, query_apart, probs, probs_wide, attended = saved
+        d_gated = pair_dot(split(grad * pair_mask), outs[t], NT)
+        d_gate = d_gated * attended * gate * (1.0 - gate)
+        d_apart = split(heads_apart(d_gated * gate))
+        d_probs = fold(pair_dot(value, d_apart, NT), at_first)
+        d_value = pair_dot(probs_wide, d_apart, NN)
+        d_logits = probs * (d_probs - jnp.sum(probs * d_probs, axis=0, keepdims=True))
+        d_wide = split(spread_over(d_logits, at_first))
+        d_key = pair_dot(d_wide, query_apart, NN)
+        d_query = heads_together(pair_dot(d_wide, key, TN)) * scale
+        d_bias = spread_over(d_logits, at_second)
+        d_all = jnp.concatenate([d_query, d_key, d_value, d_gate, d_bias], axis=1)
+        d_normed = pair_dot(split(d_all), weights, NT) * gain
+        mean_d = jnp.mean(d_normed, axis=-1, keepdims=True)
+        mean_dh = jnp.mean(d_normed * hat, axis=-1, keepdims=True)
+        return grad + inverse * (d_normed - mean_d - hat * mean_dh)
+
+    pair_two, saved_start = forward(pair_one, 0)
+    turned, saved_end = forward(turn(pair_two), 1)
+    turn_v[...] = turned
+    out_ref[0] = turn_v[pl.ds(me, count, stride=count), :]
+
+    for receive in cot_receives:
+        receive.wait_recv()
+    cot = jnp.concatenate(
+        [cot_all[:, n, :] for n in range(count)], axis=0
+    )
+    grad_two = turn(backward(cot, 1, saved_end))
+    turn_v[...] = backward(grad_two, 0, saved_start)
+    grad_ref[0] = turn_v[pl.ds(pl.multiple_of(me * count, count), count), :]
+
+    for copy in sends:
+        copy.wait_send()
+
+
+def fused_body(shape, args):
+    (
+        pair_acts,
+        alignment,
+        align_mask,
+        residue_mask,
+        align_gain,
+        outer_in,
+        outer_out,
+        tri_gain,
+        tri_in,
+        tri_bias,
+        tri_out,
+        pair_cotangent,
+    ) = args
+    rows_n, heads_n, cores_n = shape["row"], shape["head"], shape["br"]
+    count = rows_n * heads_n
+    chan = pair_acts.shape[-1]
+    seqs = alignment.shape[0]
+    half, size = tri_in.shape[2], tri_in.shape[3] // 4
+    head_count = half * cores_n
+    lanes = head_count * count * count
+    wide = 4 * head_count * size + lanes
+    others = count * cores_n
+    f32, b16 = jnp.float32, jnp.bfloat16
+    anywhere = pl.BlockSpec(memory_space=pl.ANY)
+    here = pl.BlockSpec(memory_space=pltpu.VMEM)
+    dma = pltpu.SemaphoreType.DMA
+    scratch = [
+        pltpu.VMEM((count, count + 8, chan), f32),
+        pltpu.VMEM((count, count, chan), f32),
+        pltpu.VMEM((cores_n, count, 8, (seqs // 8) * 2 * OPC), f32),
+        pltpu.VMEM(alignment.shape, f32),
+        pltpu.VMEM(align_mask.shape, jnp.int32),
+        pltpu.VMEM((1, align_gain.shape[0]), f32),
+        pltpu.VMEM(outer_in.shape, f32),
+        pltpu.VMEM(outer_out.shape, f32),
+        pltpu.VMEM(tri_gain.shape, f32),
+        pltpu.VMEM((cores_n,) + tri_in.shape, f32),
+        pltpu.VMEM((cores_n,) + tri_bias.shape, f32),
+        pltpu.VMEM((cores_n,) + tri_out.shape, f32),
+        pltpu.VMEM(outer_out.shape, b16),
+        pltpu.VMEM(outer_out.shape, b16),
+        pltpu.VMEM((2, chan, wide), b16),
+        pltpu.VMEM((2, chan, wide), b16),
+        pltpu.VMEM((count * count, chan), f32),
+        pltpu.VMEM((count * OPC // chan, count * OPC, chan), f32),
+        dma((11,)),
+        dma((others,)),
+        dma((count,)),
+        dma((others,)),
+        dma((cores_n, count)),
+        dma((others,)),
+        dma((count,)),
+        dma((3, cores_n)),
+        dma((3, cores_n)),
+    ]
+    return pl.pallas_call(
+        functools.partial(fused_kernel, (rows_n, heads_n, cores_n)),
+        out_shape=(
+            jax.ShapeDtypeStruct(pair_acts.shape, f32),
+            jax.ShapeDtypeStruct(pair_acts.shape, f32),
+        ),
+        in_specs=[pl.BlockSpec(memory_space=pltpu.SMEM)] + [anywhere] * 11,
+        out_specs=(here, here),
+        scratch_shapes=scratch,
+        compiler_params=pltpu.CompilerParams(collective_id=0, has_side_effects=True),
+    )(
+        residue_mask,
+        pair_acts,
+        alignment,
+        align_mask,
+        align_gain[None],
+        outer_in,
+        outer_out,
+        tri_gain,
+        tri_in,
+        tri_bias,
+        tri_out,
+        pair_cotangent,
+    )
+
+
+def dispatch(shape, *args):
+    pair_acts, alignment, align_mask, tri_in = args[0], args[1], args[2], args[8]
+    count = pair_acts.shape[1]
+    head_count = tri_in.shape[2] * shape["br"]
+    chan = pair_acts.shape[-1]
+    fits = (
+        pair_acts.shape[0] == 1
+        and alignment.shape[1] == 1
+        and count % 8 == 0
+        and alignment.shape[0] % 8 == 0
+        and align_mask.shape[0] <= chan
+        and head_count * (tri_in.shape[3] // 4) == chan
+        and head_count * count**4 * 4 <= FUSED_BYTES
+    )
+    return fused_body(shape, args) if fits else spread_body(*args)
+
+
 def solution(mesh):
     in_specs = (
         P(("grp", "row", "head"), None, None),
@@ -143,4 +674,4 @@
         P(("grp", "row", "head"), None, None),
     )
     out_specs = (P(("grp", "row", "head"), None, None), P(("grp", "row", "head"), None, None))
-    return jax.shard_map(body, mesh=mesh, in_specs=in_specs, out_specs=out_specs, check_vma=False)
+    return jax.shard_map(functools.partial(dispatch, dict(mesh.shape)), mesh=mesh, in_specs=in_specs, out_specs=out_specs, check_vma=False)

time: 189 us -> 23.7 us (0.13)
  blocking collectives: 135 us -> 0 us
  Pallas kernels: 0 us -> 17.2 us
  waiting for transfers between devices: 17 us -> 0 us
  starting transfers between devices: 13.2 us -> 0 us
  matrix products: 8.39 us -> 0 us
  other arithmetic: 7.59 us -> 0 us
    all_gather x4 -> x0, blocking collectives: 90 us -> none  [the longest x2 37.2 us: tri_forward(): bias_full = lax.all_gather(bias_local, ('row', 'head'), axis=1, tiled=True)]
    unnamed x2 -> x0, blocking collectives: 35.3 us -> none
    pallas_call x0 -> x1, Pallas kernels: none -> 17.2 us  [fused_body(): pl.pallas_call(functools.partial(fused_kernel, (rows_n, heads_n, cores_n)...]
    all_to_all x4 -> x0, waiting for transfers between devices: 17 us -> none  [reorient(): lax.all_to_all(turned, ('row', 'head'), split_axis=0, concat_axis=1, tile...]
    all_to_all x4 -> x0, starting transfers between devices: 13.2 us -> none  [reorient(): lax.all_to_all(turned, ('row', 'head'), split_axis=0, concat_axis=1, tile...]
    psum x4 -> x0, blocking collectives: 9.82 us -> none  [core_total(): return lax.psum(values, 'br')]
    dot_general x28 -> x0, matrix products: 8.39 us -> none  [the longest x4 2 us: prepare(): jnp.einsum('jkc,ch->hjk', normed, weight_bias, precision=PRECISE)]
    add x4 -> x0, other arithmetic: 2.52 us -> none  [the longest x2 1.33 us: tri_forward(): return (rows_in + total_out * pair_mask, (pull_prep, pull_attend))]
  transfers between devices with their start and end apart: 4 -> 0, of which waited for: 3 -> 0; matrix products, arithmetic and copies ran while one was open for 2% -> 0% of each run, Pallas kernels for 0% -> 0%
where the time goes in v1:
time: 23.7 us; the launch traced here: 23.5 us
  Pallas kernels  17.2 us (73%)
  local copies, waits for them, and re-layouts  5.58 us (24%)
  between operations  0.66 us (3%)
    pallas_call x1, Pallas kernels, fused_body(): pl.pallas_call(functools.partial(fused_kernel, (rows_n, heads_n, cores_n)...  17.2 us
    unnamed x11, local copies, waits for them, and re-layouts  5.58 us

profile of v1, /device:TPU:0, one launch (start us, length us, event | category | flops | bytes accessed | tf_op | source)
XLA Modules:
  0.0 23.5 jit_solution(4850784557136664192)
XLA Ops:
  0.6 0.0 copy-start.2
  0.6 0.6 %copy-done.2 = s32[32,1]{0,1:T(1,128)S(1)} copy-done((s32[32,1]{0,1:T(1,128)S(1)}, s32[32,1]{0,1:T(1,128)}, u32[]{:S(2)}) %copy-start.2) | copy-done | bytes 152
  1.3 0.7 %copy.14.mask_hbm = s32[32,1]{1,0:T(8,128)} copy(s32[32,1]{0,1:T(1,128)S(1)} %copy-done.2) | data formatting | bytes 256 | tf_op args[2]
  2.0 0.0 copy-start.1
  2.0 1.6 %copy.15.outer_in_hbm = f32[256,64]{1,0:T(8,128)} copy(f32[256,64]{0,1:T(8,128)} %param.17) | data formatting | bytes 131072 | tf_op args[5]
  3.6 0.0 copy-done.1
  3.6 0.8 %copy.16.tri_bias_hbm = f32[2,128,2]{2,1,0:T(8,128)} copy(f32[2,128,2]{1,2,0:T(2,128)S(1)} %copy-done.1) | data formatting | bytes 4096 | tf_op args[9]
  4.4 17.2 %shard_map.131 = (f32[1,8,128]{2,1,0:T(8,128)}, f32[1,8,128]{2,1,0:T(8,128)}) custom-call(s32[8]{0:T(128)} %live_ref.1, f32[1,8,128]{2,1,0:T(8,128)} %acts_hbm.1, f32[16,1,256]{2,1,0:T(1,128)} %align_hbm.1, s32[32,1]{1,0:T(8,128)} %copy.14.mask_hbm, f32[1,256]{1,0:T(1,128)} %bitcast.1, f32[256,64]{1,0:T(8,128)} %copy.15.outer_in_hbm, ...), custom_call_target="tpu_custom_call" | custom-call | tf_op jit(solution)/shard_map/pallas_call | solution.py:618
  21.6 0.0 copy-start
  21.6 1.3 %copy.19 = f32[1,8,128]{2,1,0:T(8,128)} copy(f32[1,8,128]{2,1,0:T(8,128)} %get-tuple-element.4) | data formatting | bytes 8192
  22.9 0.0 copy-done
  22.9 0.6 %copy.20 = f32[1,8,128]{2,1,0:T(8,128)} copy(f32[1,8,128]{2,1,0:T(8,128)S(1)} %copy-done) | data formatting | bytes 8192
Async XLA Ops:
  0.6 0.7 %copy-start.2 = (s32[32,1]{0,1:T(1,128)S(1)}, s32[32,1]{0,1:T(1,128)}, u32[]{:S(2)}) copy-start(s32[32,1]{0,1:T(1,128)} %param.14) | copy-start | bytes 388
  2.0 1.6 %copy-start.1 = (f32[2,128,2]{1,2,0:T(2,128)S(1)}, f32[2,128,2]{1,2,0:T(2,128)}, u32[]{:S(2)}) copy-start(f32[2,128,2]{1,2,0:T(2,128)} %param.21) | copy-start | bytes 6148
  21.6 1.3 %copy-start = (f32[1,8,128]{2,1,0:T(8,128)S(1)}, f32[1,8,128]{2,1,0:T(8,128)}, u32[]{:S(2)}) copy-start(f32[1,8,128]{2,1,0:T(8,128)} %get-tuple-element.5) | copy-start | bytes 12292

commit v2 on v1

--- a/solution.py
+++ b/solution.py
@@ -174,7 +174,6 @@
     tri_out_hbm,
     cot_hbm,
     out_ref,
-    grad_ref,
     acts_all,
     cot_all,
     proj_all,
@@ -260,22 +259,20 @@
 
     aligned = align_v[:, 0, :]
     normed = standardize(aligned)[0] * gain_v[...]
-    projected = pair_dot(split(normed), split(outer_in_v[...]), NN)
+    projected = pair_dot(split(normed), split(outer_in_v[...]), NT)
     mask_f = mask_v[...].astype(jnp.float32)
-    lo_seq = mask_f[0:seqs]
-    mask_own = lo_seq
-    for core in range(1, cores_n):
-        mask_own = jnp.where(my_core == core, mask_f[core * seqs : (core + 1) * seqs], mask_own)
+    depth = mask_f.shape[1]
+    lane = lax.broadcasted_iota(jnp.int32, (seqs, depth), 1)
+    own_s = lax.broadcasted_iota(jnp.int32, (seqs, depth), 0) + my_core * seqs
+    mask_own = jnp.sum(jnp.where(lane == own_s, mask_f, 0.0), axis=1, keepdims=True)
     projected = projected * mask_own
     pieces = seqs // 8
     proj_all[my_core, me] = jnp.concatenate(
         [projected[8 * piece : 8 * piece + 8] for piece in range(pieces)], axis=1
     )
-    depth = mask_f.shape[0]
-    lane = lax.broadcasted_iota(jnp.int32, (depth, chan), 1)
-    place_s = lax.broadcasted_iota(jnp.int32, (depth, chan), 0)
-    mask_row = jnp.sum(jnp.where(lane == place_s, mask_f, 0.0), axis=0, keepdims=True)
-    acts_all[me, count : count + 1] = mask_row
+    acts_all[me, count : count + 1] = jnp.concatenate(
+        [mask_f, jnp.zeros((1, chan - depth), jnp.float32)], axis=1
+    )
     for load in loads[4:]:
         load.wait()
 
@@ -436,11 +433,15 @@
             high, low = split(columns)
             wide_hi[t, :, block * width : (block + 1) * width] = high
             wide_lo[t, :, block * width : (block + 1) * width] = low
+        bias_rows = jnp.concatenate(
+            [tri_bias_all[core, t] for core in range(cores_n)]
+            + [jnp.zeros((chan - head_count, chan), jnp.float32)],
+            axis=0,
+        )
+        bias_turned = bias_rows.T
         bias_columns = jnp.concatenate(
             [
-                jnp.broadcast_to(
-                    tri_bias_all[h // half, t, :, h % half : h % half + 1], (chan, pairs)
-                )
+                jnp.broadcast_to(bias_turned[:, h : h + 1], (chan, pairs))
                 for h in range(head_count)
             ],
             axis=1,
@@ -552,7 +553,7 @@
     )
     grad_two = turn(backward(cot, 1, saved_end))
     turn_v[...] = backward(grad_two, 0, saved_start)
-    grad_ref[0] = turn_v[pl.ds(pl.multiple_of(me * count, count), count), :]
+    out_ref[1] = turn_v[pl.ds(pl.multiple_of(me * count, count), count), :]
 
     for copy in sends:
         copy.wait_send()
@@ -591,13 +592,13 @@
         pltpu.VMEM((count, count, chan), f32),
         pltpu.VMEM((cores_n, count, 8, (seqs // 8) * 2 * OPC), f32),
         pltpu.VMEM(alignment.shape, f32),
-        pltpu.VMEM(align_mask.shape, jnp.int32),
+        pltpu.VMEM(align_mask.shape[::-1], jnp.int32),
         pltpu.VMEM((1, align_gain.shape[0]), f32),
-        pltpu.VMEM(outer_in.shape, f32),
+        pltpu.VMEM(outer_in.shape[::-1], f32),
         pltpu.VMEM(outer_out.shape, f32),
         pltpu.VMEM(tri_gain.shape, f32),
         pltpu.VMEM((cores_n,) + tri_in.shape, f32),
-        pltpu.VMEM((cores_n,) + tri_bias.shape, f32),
+        pltpu.VMEM((cores_n, 2, half, chan), f32),
         pltpu.VMEM((cores_n,) + tri_out.shape, f32),
         pltpu.VMEM(outer_out.shape, b16),
         pltpu.VMEM(outer_out.shape, b16),
@@ -615,30 +616,28 @@
         dma((3, cores_n)),
         dma((3, cores_n)),
     ]
-    return pl.pallas_call(
+    both = pl.pallas_call(
         functools.partial(fused_kernel, (rows_n, heads_n, cores_n)),
-        out_shape=(
-            jax.ShapeDtypeStruct(pair_acts.shape, f32),
-            jax.ShapeDtypeStruct(pair_acts.shape, f32),
-        ),
+        out_shape=jax.ShapeDtypeStruct((2,) + pair_acts.shape[1:], f32),
         in_specs=[pl.BlockSpec(memory_space=pltpu.SMEM)] + [anywhere] * 11,
-        out_specs=(here, here),
+        out_specs=here,
         scratch_shapes=scratch,
         compiler_params=pltpu.CompilerParams(collective_id=0, has_side_effects=True),
     )(
         residue_mask,
         pair_acts,
         alignment,
-        align_mask,
+        align_mask.T,
         align_gain[None],
-        outer_in,
+        outer_in.T,
         outer_out,
         tri_gain,
         tri_in,
-        tri_bias,
+        jnp.swapaxes(tri_bias, 1, 2),
         tri_out,
         pair_cotangent,
     )
+    return (both[0:1], both[1:2])
 
 
 def dispatch(shape, *args):

time: 23.7 us -> 19.4 us (0.82)
  local copies, waits for them, and re-layouts: 5.58 us -> 1.28 us
    unnamed x11 -> x0, local copies, waits for them, and re-layouts: 5.58 us -> none
    slice x0 -> x1, local copies, waits for them, and re-layouts: none -> 1.28 us  [fused_body(): return (both[0:1], both[1:2])]
where the time goes in v2:
time: 19.4 us; the launch traced here: 19.1 us
  Pallas kernels  17.2 us (89%)
  local copies, waits for them, and re-layouts  1.28 us (7%)
  between operations  0.64 us (3%)
    pallas_call x1, Pallas kernels, fused_body(): pl.pallas_call(functools.partial(fused_kernel, (rows_n, heads_n, cores_n)...  17.2 us
    slice x1, local copies, waits for them, and re-layouts, fused_body(): return (both[0:1], both[1:2])  1.28 us

profile of v2, /device:TPU:0, one launch (start us, length us, event | category | flops | bytes accessed | tf_op | source)
XLA Modules:
  0.0 19.1 jit_solution(7197184604207567948)
XLA Ops:
  0.6 17.2 %shard_map.131 = f32[2,8,128]{2,1,0:T(8,128)} custom-call(s32[8]{0:T(128)} %live_ref.1, f32[1,8,128]{2,1,0:T(8,128)} %acts_hbm.1, f32[16,1,256]{2,1,0:T(1,128)} %align_hbm.1, s32[1,32]{1,0:T(1,128)} %bitcast.7, f32[1,256]{1,0:T(1,128)} %bitcast.6, f32[64,256]{1,0:T(8,128)} %bitcast.4, f32[1024,128]{1,0:T(8,128)} %outer_out_hbm.1, f32[2,128]{1,0:T(2,128)} %tri_gain_hbm.1, ...), custom_call_target="tpu_custom_call" | custom-call | tf_op jit(solution)/shard_map/pallas_call | solution.py:619
  17.8 1.3 %fusion = (f32[1,8,128]{2,1,0:T(8,128)}, f32[1,8,128]{2,1,0:T(8,128)}) fusion(f32[2,8,128]{2,1,0:T(8,128)} %shard_map.131), kind=kLoop, calls=%fused_computation | loop fusion | bytes 16384 | tf_op jit(solution)/shard_map/slice | solution.py:640

commit v3 on v2

--- a/solution.py
+++ b/solution.py
@@ -148,7 +148,9 @@
     def one(a, b):
         return lax.dot_general(a, b, (dims, ((), ())), preferred_element_type=jnp.float32)
 
-    return one(first[0], second[0]) + (one(first[0], second[1]) + one(first[1], second[0]))
+    a = jnp.concatenate([first[0], first[1], first[0]], axis=dims[0][0])
+    b = jnp.concatenate([second[0], second[0], second[1]], axis=dims[1][0])
+    return one(a, b)
 
 
 def standardize(values):
@@ -174,9 +176,8 @@
     tri_out_hbm,
     cot_hbm,
     out_ref,
-    acts_all,
+    block_all,
     cot_all,
-    proj_all,
     align_v,
     mask_v,
     gain_v,
@@ -193,10 +194,8 @@
     turn_v,
     mixed_v,
     load_sems,
-    send_acts,
-    recv_acts,
-    send_proj,
-    recv_proj,
+    send_block,
+    recv_block,
     send_cot,
     recv_cot,
     send_w,
@@ -204,7 +203,7 @@
 ):
     rows_n, heads_n, cores_n = sizes
     count = rows_n * heads_n
-    chan = acts_all.shape[-1]
+    chan = cot_all.shape[-1]
     my_row = lax.axis_index("row")
     my_head = lax.axis_index("head")
     my_core = lax.axis_index("br")
@@ -244,7 +243,7 @@
         pltpu.make_async_copy(gain_hbm, gain_v, load_sems.at[1]),
         pltpu.make_async_copy(outer_in_hbm, outer_in_v, load_sems.at[2]),
         pltpu.make_async_copy(mask_hbm, mask_v, load_sems.at[3]),
-        pltpu.make_async_copy(acts_hbm.at[0], acts_all.at[me, 0:count], load_sems.at[4]),
+        pltpu.make_async_copy(acts_hbm.at[0], block_all.at[my_core, me, 0:count], load_sems.at[4]),
         pltpu.make_async_copy(tri_in_hbm, tri_in_all.at[my_core], load_sems.at[5]),
         pltpu.make_async_copy(tri_bias_hbm, tri_bias_all.at[my_core], load_sems.at[6]),
         pltpu.make_async_copy(tri_out_hbm, tri_out_all.at[my_core], load_sems.at[7]),
@@ -267,10 +266,10 @@
     mask_own = jnp.sum(jnp.where(lane == own_s, mask_f, 0.0), axis=1, keepdims=True)
     projected = projected * mask_own
     pieces = seqs // 8
-    proj_all[my_core, me] = jnp.concatenate(
+    block_all[my_core, me, count : count + 8] = jnp.concatenate(
         [projected[8 * piece : 8 * piece + 8] for piece in range(pieces)], axis=1
     )
-    acts_all[me, count : count + 1] = jnp.concatenate(
+    block_all[my_core, me, count + 8 : count + 9] = jnp.concatenate(
         [mask_f, jnp.zeros((1, chan - depth), jnp.float32)], axis=1
     )
     for load in loads[4:]:
@@ -297,43 +296,15 @@
     for number, offset in enumerate(ordered):
         row, head, core = place(offset)
         other = row * heads_n + head
-        copy = remote(
-            proj_all.at[my_core, me],
-            proj_all.at[my_core, me],
-            send_proj.at[number],
-            recv_proj.at[my_core, me],
-            offset,
-        )
+        span = slice(0, count + 9) if offset[2] == 0 else slice(count, count + 8)
+        mine = block_all.at[my_core, me, span]
+        theirs = block_all.at[core, other, span]
+        copy = remote(mine, mine, send_block.at[number], recv_block.at[my_core, me], offset)
         copy.start()
         sends.append(copy)
         receives.append(
-            remote(
-                proj_all.at[core, other],
-                proj_all.at[core, other],
-                send_proj.at[number],
-                recv_proj.at[core, other],
-                offset,
-            )
-        )
-        if offset[2] == 0:
-            copy = remote(
-                acts_all.at[me, 0 : count + 1],
-                acts_all.at[me, 0 : count + 1],
-                send_acts.at[number],
-                recv_acts.at[me],
-                offset,
-            )
-            copy.start()
-            sends.append(copy)
-            receives.append(
-                remote(
-                    acts_all.at[other, 0 : count + 1],
-                    acts_all.at[other, 0 : count + 1],
-                    send_acts.at[number],
-                    recv_acts.at[other],
-                    offset,
-                )
-            )
+            remote(theirs, theirs, send_block.at[number], recv_block.at[core, other], offset)
+        )
     for db in range(1, cores_n):
         offset = (0, 0, db)
         core = lax.rem(my_core + db, cores_n)
@@ -467,12 +438,15 @@
             base = piece * 2 * OPC
             left_tiles.append(
                 jnp.concatenate(
-                    [proj_all[core, n, :, base : base + OPC] for n in range(count)], axis=1
+                    [block_all[core, n, count : count + 8, base : base + OPC] for n in range(count)], axis=1
                 )
             )
             right_tiles.append(
                 jnp.concatenate(
-                    [proj_all[core, n, :, base + OPC : base + 2 * OPC] for n in range(count)],
+                    [
+                        block_all[core, n, count : count + 8, base + OPC : base + 2 * OPC]
+                        for n in range(count)
+                    ],
                     axis=1,
                 )
             )
@@ -489,9 +463,11 @@
                 strips[block * (chan // OPC) + n].append(tile[:, n * OPC : (n + 1) * OPC])
     crossed = jnp.concatenate([jnp.concatenate(s, axis=1) for s in strips], axis=0)
     summed = pair_dot(split(crossed), (table_hi[...], table_lo[...]), NN)
-    mask_rows = jnp.concatenate([acts_all[n, count : count + 1] for n in range(count)], axis=0)
+    mask_rows = jnp.concatenate(
+        [block_all[my_core, n, count + 8 : count + 9] for n in range(count)], axis=0
+    )
     counts = jnp.sum(mask_rows[:, None, :] * mask_rows[None, :, :], axis=-1, keepdims=True)
-    acts = jnp.concatenate([acts_all[n, 0:count] for n in range(count)], axis=0)
+    acts = jnp.concatenate([block_all[my_core, n, 0:count] for n in range(count)], axis=0)
     pair_one = acts + summed / counts.reshape(pairs, 1)
 
     def turn(values):
@@ -588,9 +564,8 @@
     here = pl.BlockSpec(memory_space=pltpu.VMEM)
     dma = pltpu.SemaphoreType.DMA
     scratch = [
-        pltpu.VMEM((count, count + 8, chan), f32),
+        pltpu.VMEM((cores_n, count, count + 16, chan), f32),
         pltpu.VMEM((count, count, chan), f32),
-        pltpu.VMEM((cores_n, count, 8, (seqs // 8) * 2 * OPC), f32),
         pltpu.VMEM(alignment.shape, f32),
         pltpu.VMEM(align_mask.shape[::-1], jnp.int32),
         pltpu.VMEM((1, align_gain.shape[0]), f32),
@@ -608,8 +583,6 @@
         pltpu.VMEM((count * OPC // chan, count * OPC, chan), f32),
         dma((11,)),
         dma((others,)),
-        dma((count,)),
-        dma((others,)),
         dma((cores_n, count)),
         dma((others,)),
         dma((count,)),
@@ -618,7 +591,7 @@
     ]
     both = pl.pallas_call(
         functools.partial(fused_kernel, (rows_n, heads_n, cores_n)),
-        out_shape=jax.ShapeDtypeStruct((2,) + pair_acts.shape[1:], f32),
+        out_shape=pltpu.VMEM((2,) + pair_acts.shape[1:], f32),
         in_specs=[pl.BlockSpec(memory_space=pltpu.SMEM)] + [anywhere] * 11,
         out_specs=here,
         scratch_shapes=scratch,
@@ -649,7 +622,7 @@
         pair_acts.shape[0] == 1
         and alignment.shape[1] == 1
         and count % 8 == 0
-        and alignment.shape[0] % 8 == 0
+        and alignment.shape[0] // 8 * 2 * OPC == chan
         and align_mask.shape[0] <= chan
         and head_count * (tri_in.shape[3] // 4) == chan
         and head_count * count**4 * 4 <= FUSED_BYTES

time: 19.4 us -> 17.3 us (0.89)
  Pallas kernels: 17.2 us -> 15.8 us
  local copies, waits for them, and re-layouts: 1.28 us -> 0.6 us
    pallas_call x1, Pallas kernels: 17.2 us -> 15.8 us  [fused_body(): pl.pallas_call(functools.partial(fused_kernel, (rows_n, heads_n, cores_n)...]
    slice x1, local copies, waits for them, and re-layouts: 1.28 us -> 0.6 us  [fused_body(): return (both[0:1], both[1:2])]
where the time goes in v3:
time: 17.3 us; the launch traced here: 17 us
  Pallas kernels  15.8 us (91%)
  between operations  0.64 us (4%)
  local copies, waits for them, and re-layouts  0.6 us (3%)
    pallas_call x1, Pallas kernels, fused_body(): pl.pallas_call(functools.partial(fused_kernel, (rows_n, heads_n, cores_n)...  15.8 us
    slice x1, local copies, waits for them, and re-layouts, fused_body(): return (both[0:1], both[1:2])  0.6 us

profile of v3, /device:TPU:0, one launch (start us, length us, event | category | flops | bytes accessed | tf_op | source)
XLA Modules:
  0.0 17.0 jit_solution(16006881139125273969)
XLA Ops:
  0.6 15.8 %shard_map.131 = f32[2,8,128]{2,1,0:T(8,128)S(1)} custom-call(s32[8]{0:T(128)} %live_ref.1, f32[1,8,128]{2,1,0:T(8,128)} %acts_hbm.1, f32[16,1,256]{2,1,0:T(1,128)} %align_hbm.1, s32[1,32]{1,0:T(1,128)} %bitcast.7, f32[1,256]{1,0:T(1,128)} %bitcast.6, f32[64,256]{1,0:T(8,128)} %bitcast.4, f32[1024,128]{1,0:T(8,128)} %outer_out_hbm.1, f32[2,128]{1,0:T(2,128)} %tri_gain_hbm.1, ...), custom_call_target="tpu_custom_call" | custom-call | tf_op jit(solution)/shard_map/pallas_call | solution.py:592
  16.4 0.6 %fusion = (f32[1,8,128]{2,1,0:T(8,128)}, f32[1,8,128]{2,1,0:T(8,128)}) fusion(f32[2,8,128]{2,1,0:T(8,128)S(1)} %shard_map.131), kind=kLoop, calls=%fused_computation | loop fusion | bytes 16384 | tf_op jit(solution)/shard_map/slice | solution.py:613

commit v4 on v3

--- a/solution.py
+++ b/solution.py
@@ -499,9 +499,11 @@
         saved = (hat, inverse, gain, weights, key, value, gate, query_apart, probs, probs_wide, attended)
         return (x + update * pair_mask, saved)
 
-    def backward(grad, t, saved):
+    def gated_of(grad, t):
+        return pair_dot(split(grad * pair_mask), outs[t], NT)
+
+    def backward(grad, d_gated, t, saved):
         hat, inverse, gain, weights, key, value, gate, query_apart, probs, probs_wide, attended = saved
-        d_gated = pair_dot(split(grad * pair_mask), outs[t], NT)
         d_gate = d_gated * attended * gate * (1.0 - gate)
         d_apart = split(heads_apart(d_gated * gate))
         d_probs = fold(pair_dot(value, d_apart, NT), at_first)
@@ -511,24 +513,29 @@
         d_key = pair_dot(d_wide, query_apart, NN)
         d_query = heads_together(pair_dot(d_wide, key, TN)) * scale
         d_bias = spread_over(d_logits, at_second)
-        d_all = jnp.concatenate([d_query, d_key, d_value, d_gate, d_bias], axis=1)
-        d_normed = pair_dot(split(d_all), weights, NT) * gain
+
+        def through(values, start, stop):
+            return pair_dot(split(values), (weights[0][:, start:stop], weights[1][:, start:stop]), NT)
+
+        early = through(jnp.concatenate([d_value, d_gate], axis=1), 2 * width, 4 * width)
+        middle = through(d_bias, 4 * width, 4 * width + lanes)
+        late = through(jnp.concatenate([d_query, d_key], axis=1), 0, 2 * width)
+        d_normed = (early + middle + late) * gain
         mean_d = jnp.mean(d_normed, axis=-1, keepdims=True)
         mean_dh = jnp.mean(d_normed * hat, axis=-1, keepdims=True)
         return grad + inverse * (d_normed - mean_d - hat * mean_dh)
 
     pair_two, saved_start = forward(pair_one, 0)
+    for receive in cot_receives:
+        receive.wait_recv()
+    cot = jnp.concatenate([cot_all[:, n, :] for n in range(count)], axis=0)
+    cot_gated = gated_of(cot, 1)
     turned, saved_end = forward(turn(pair_two), 1)
     turn_v[...] = turned
     out_ref[0] = turn_v[pl.ds(me, count, stride=count), :]
 
-    for receive in cot_receives:
-        receive.wait_recv()
-    cot = jnp.concatenate(
-        [cot_all[:, n, :] for n in range(count)], axis=0
-    )
-    grad_two = turn(backward(cot, 1, saved_end))
-    turn_v[...] = backward(grad_two, 0, saved_start)
+    grad_two = turn(backward(cot, cot_gated, 1, saved_end))
+    turn_v[...] = backward(grad_two, gated_of(grad_two, 0), 0, saved_start)
     out_ref[1] = turn_v[pl.ds(pl.multiple_of(me * count, count), count), :]
 
     for copy in sends:

time: 17.3 us -> 16.8 us (0.971)
  Pallas kernels: 15.8 us -> 15.3 us
    pallas_call x1, Pallas kernels: 15.8 us -> 15.3 us  [fused_body(): pl.pallas_call(functools.partial(fused_kernel, (rows_n, heads_n, cores_n)...]
where the time goes in v4:
time: 16.8 us; the launch traced here: 16.6 us
  Pallas kernels  15.3 us (91%)
  between operations  0.64 us (4%)
  local copies, waits for them, and re-layouts  0.6 us (4%)
    pallas_call x1, Pallas kernels, fused_body(): pl.pallas_call(functools.partial(fused_kernel, (rows_n, heads_n, cores_n)...  15.3 us
    slice x1, local copies, waits for them, and re-layouts, fused_body(): return (both[0:1], both[1:2])  0.6 us

profile of v4, /device:TPU:0, one launch (start us, length us, event | category | flops | bytes accessed | tf_op | source)
XLA Modules:
  0.0 16.6 jit_solution(6413270751110931227)
XLA Ops:
  0.6 15.3 %shard_map.131 = f32[2,8,128]{2,1,0:T(8,128)S(1)} custom-call(s32[8]{0:T(128)} %live_ref.1, f32[1,8,128]{2,1,0:T(8,128)} %acts_hbm.1, f32[16,1,256]{2,1,0:T(1,128)} %align_hbm.1, s32[1,32]{1,0:T(1,128)} %bitcast.7, f32[1,256]{1,0:T(1,128)} %bitcast.6, f32[64,256]{1,0:T(8,128)} %bitcast.4, f32[1024,128]{1,0:T(8,128)} %outer_out_hbm.1, f32[2,128]{1,0:T(2,128)} %tri_gain_hbm.1, ...), custom_call_target="tpu_custom_call" | custom-call | tf_op jit(solution)/shard_map/pallas_call | solution.py:599
  16.0 0.6 %fusion = (f32[1,8,128]{2,1,0:T(8,128)}, f32[1,8,128]{2,1,0:T(8,128)}) fusion(f32[2,8,128]{2,1,0:T(8,128)S(1)} %shard_map.131), kind=kLoop, calls=%fused_computation | loop fusion | bytes 16384 | tf_op jit(solution)/shard_map/slice | solution.py:620
